TPU v7x, 256 devices: a whole 4x4x8 slice. The times are simulated.
256 devices in a mesh: group: 8 (over z), ghost: 32 (over x, y, core).
Axes of the slice: x: 4, y: 4, z: 8, core: 2. Of those that a mesh axis runs over, the one named last changes fastest.
Arguments:
- inputs: bfloat16 [200704, 1024], P(('group', 'ghost')), may hold values from -24 to 24
- out_grad: bfloat16 [200704, 1024], P(('group', 'ghost')), may hold values from -6 to 6
- conv_first: bfloat16 [1024, 256], replicated, may hold values from -0.25 to 0.25
- conv_middle: bfloat16 [2304, 256], replicated, may hold values from -0.1875 to 0.1875
- conv_last: bfloat16 [256, 1024], replicated, may hold values from -0.375 to 0.375
- gain: float32 [1024], replicated, may hold values from 0.5 to 1.5
Outputs:
- input_grad: bfloat16 [200704, 1024], P(('group', 'ghost'))
- first_grad: float32 [262144], P(('group', 'ghost'))
- middle_grad: float32 [589824], P(('group', 'ghost'))
- last_grad: float32 [262144], P(('group', 'ghost'))
- gain_grad: float32 [1024], P(('group', 'ghost'))
All inputs are finite; a program needn't handle non-finite values.
Results may differ from a plain program's by a relative error of at most 0.0071.
Values sent between devices are 32-bit elements; how exact they have to be, the bound alone decides.
A program may use at most 128 MiB of HBM per device.

v0:
```python
import jax
import jax.numpy as jnp
from jax import lax
from jax.experimental import pallas as pl
from jax.experimental.pallas import tpu as pltpu
from jax.sharding import PartitionSpec as P

GROUP = 64
NEWTON = 5
SIDE = 14
PAD = 16
TILE = 112
MESH = pl.DeviceIdType.MESH
epsilon = 1e-05
F32 = jnp.float32
BF16 = jnp.bfloat16


def dot(left, right, dims=((1,), (0,))):
    return lax.dot_general(left, right, (dims, ((), ())), preferred_element_type=F32)


def parts(value, count):
    pieces = []
    for _ in range(count):
        piece = value.astype(BF16)
        pieces.append(piece)
        value = value - piece.astype(F32)
    return pieces


def dot_parts(left, right, dims=((1,), (0,))):
    total = None
    for a in left:
        for b in right:
            term = dot(a, b, dims)
            total = term if total is None else total + term
    return total


def dot_high(left, right, dims=((1,), (0,))):
    return lax.dot_general(
        left, right, (dims, ((), ())), preferred_element_type=F32, precision=lax.Precision.HIGHEST
    )


def tile_rows(t):
    return pl.ds(pl.multiple_of(t * TILE, TILE), TILE)


def edges(t):
    row = lax.broadcasted_iota(jnp.int32, (TILE, 256), 0).astype(F32) + float(t * TILE)
    line = jnp.floor((row + 0.5) * (1.0 / SIDE))
    column = row - line * SIDE
    image = jnp.floor((line + 0.5) * (1.0 / SIDE))
    return line - image * SIDE, column


def shifted_tiles(padded, columns, sign):
    for t in range(columns.shape[0] // TILE):
        line, column = edges(t)
        at = slice(t * TILE, t * TILE + TILE)
        for tap in range(9):
            dr, dc = sign * (tap // 3 - 1), sign * (tap % 3 - 1)
            start = t * TILE + PAD + dr * SIDE + dc
            value = padded[start : start + TILE, :]
            keep = None
            if dr:
                keep = line > 0.5 if dr < 0 else line < SIDE - 1.5
            if dc:
                side = column > 0.5 if dc < 0 else column < SIDE - 1.5
                keep = side if keep is None else keep & side
            if keep is not None:
                value = jnp.where(keep, value, 0.0)
            columns[at, tap * 256 : tap * 256 + 256] = value.astype(BF16)


def lanes_of(rows, right):
    lane = lax.broadcasted_iota(jnp.int32, (rows, 128), 1)
    return lane, lane - (64 if right else 0), lax.broadcasted_iota(jnp.int32, (rows, 128), 0)


def pack_block(square, at, right, row):
    top, low = square[at : at + 32], square[at + 32 : at + 64]
    lane, rel, i = lanes_of(32, right)
    moved = pltpu.roll(low, 96, 1)
    corner = jnp.where(rel > i, top, jnp.where(rel == i, 0.5 * top, moved))
    value = jnp.where(rel < 32, corner, top)
    upper, lower = value[:16], value[16:]
    if right:
        upper = pltpu.roll(upper, 64, 1)
    else:
        lower = pltpu.roll(lower, 64, 1)
    packed = jnp.where(lane[:16] < 64, upper, lower)
    diagonal = jnp.sum(jnp.where(rel - 32 == i, 0.5 * low, 0.0), axis=0, keepdims=True)
    diagonal = pltpu.roll(diagonal, 96 if right else 32, 1)
    if right:
        row = pltpu.roll(row, 64, 1)
    flat = lane[:1]
    return packed, jnp.where(flat < 64, row, jnp.where(flat < 96, diagonal, 0.0))


def half_block(packed, extra, right):
    lane, rel, i = lanes_of(32, right)
    rolled = pltpu.roll(packed, 64, 1)
    value = jnp.concatenate([rolled, packed] if right else [packed, rolled], axis=0)
    diagonal = pltpu.roll(extra, 32 if right else 96, 1)
    inside = (rel >= 0) & (rel < 64)
    top = jnp.where(inside & ((rel >= 32) | (rel >= i)), value, 0.0)
    low = jnp.where(inside & (rel >= 32) & (rel - 32 < i), pltpu.roll(value, 32, 1), 0.0)
    low = jnp.where(rel - 32 == i, diagonal, low)
    return top, low


def fill_diagonal(target, source):
    zero = jnp.zeros((128, 128), F32)
    for pair in range(8):
        j, at = pair // 2, (pair % 2) * 128
        pieces = []
        for right in (False, True):
            k = 2 * pair + int(right)
            pieces += half_block(source[k, :16, :], source[k, 16:17, :], right)
        half = jnp.concatenate(pieces, axis=0)
        target[j, at : at + 128, at : at + 128] = half + half.T
        target[j, at : at + 128, 128 - at : 256 - at] = zero


def fill_row(target, source):
    lane = lax.broadcasted_iota(jnp.int32, (1, 128), 1)
    for pair in range(8):
        right = pltpu.roll(source[2 * pair + 1, 16:17, :], 64, 1)
        target[0:1, pair * 128 : pair * 128 + 128] = jnp.where(lane < 64, source[2 * pair, 16:17, :], right)


def fill_payload(payload, squares, row):
    for j in range(4):
        square = squares(j)
        for q in range(4):
            k = 4 * j + q
            tile = (q // 2) * 128
            packed, extra = pack_block(
                square[:, tile : tile + 128], q * 64, bool(q % 2), row[:, (k // 2) * 128 : (k // 2) * 128 + 128]
            )
            payload[k, :16, :] = packed
            payload[k, 16:17, :] = extra


def block_of(packed, extra):
    top, low = half_block(packed, extra, False)
    half = jnp.concatenate([top, low], axis=0)[:, :64]
    return half + half.T


def packed_of(square, row):
    wide = jnp.concatenate([square, jnp.zeros((64, 64), F32)], axis=1)
    return pack_block(wide, 0, False, jnp.concatenate([row, jnp.zeros((1, 64), F32)], axis=1))


def outer(left, right):
    first = lax.broadcasted_iota(jnp.int32, (8, 64), 0) == 0
    return dot_high(jnp.where(first, left, 0.0), jnp.broadcast_to(right, (8, 64)), ((0,), (0,)))


def eye(size):
    return lax.broadcasted_iota(jnp.int32, (size, size), 0) == lax.broadcasted_iota(jnp.int32, (size, size), 1)


def solve_white(span, packed, extra, keep):
    mean = extra[:, :64] * (1.0 / span)
    cov = block_of(packed, extra) * (1.0 / span) - outer(mean, mean) + jnp.where(eye(64), epsilon, 0.0)
    trace = trace_of(cov)
    white = newton(cov / trace, 64) / jnp.sqrt(jnp.full((64, 64), trace))
    keep[:64] = cov
    keep[64:128] = white
    keep[128:136] = jnp.broadcast_to(mean, (8, 64))
    return packed_of(white, dot_high(jnp.broadcast_to(mean, (8, 64)), white)[:1])


def solve_slope(span, packed, extra, keep):
    cov, white, mean = keep[:64], keep[64:128], keep[128:129]
    csum = extra[:, :64]
    lifted = outer(mean, csum)
    cross = block_of(packed, extra) - 0.5 * (lifted + lifted.T)
    trace = trace_of(cov)
    scaled = cov / trace
    up = jnp.concatenate([scaled, cross / jnp.sqrt(jnp.full((64, 64), trace))], axis=1)
    low = jnp.concatenate([jnp.zeros((64, 64), F32), scaled], axis=1)
    dn = newton(jnp.concatenate([up, low], axis=0), 128)[:64, 64:]
    dt = -jnp.sum(dn * scaled) / trace - 0.5 * jnp.sum(cross * white) / trace
    dcov = dn / trace + jnp.where(eye(64), dt, 0.0)
    sym = dcov + dcov.T
    wide = jnp.broadcast_to(csum, (8, 64))
    line = dot_high(wide, white, ((1,), (1,))) + dot_high(jnp.broadcast_to(mean, (8, 64)), sym)
    return packed_of(sym, line[:1] * (1.0 / span))


def remote(source, target, sems, at, peer):
    send, recv = sems
    return pltpu.make_async_remote_copy(
        src_ref=source, dst_ref=target, send_sem=send.at[at], recv_sem=recv.at[at], device_id=peer,
        device_id_type=MESH,
    )


class Place:
    def __init__(self):
        self.z, ghost = lax.axis_index("group"), lax.axis_index("ghost")
        self.x, self.y, self.core, self.chip = ghost // 8, (ghost // 2) % 4, ghost % 2, ghost // 2

    def chip_peer(self, chip):
        return (self.z, chip * 2 + self.core)

    def partner(self):
        return (self.z, self.chip * 2 + 1 - self.core)

    def along_x(self, s):
        return (self.z, ((self.x + s + 4) % 4) * 8 + self.y * 2 + self.core)

    def along_y(self, s):
        return (self.z, self.x * 8 + ((self.y + s + 4) % 4) * 2 + self.core)

    def along_z(self, s):
        return ((self.z + s) % 8, self.chip * 2 + self.core)

    def greet(self):
        barrier = pltpu.get_barrier_semaphore()

        def signal(peer):
            pl.semaphore_signal(barrier, inc=1, device_id=peer, device_id_type=MESH)

        for s in range(1, 16):
            signal(self.chip_peer((self.chip + s) % 16))
        for s in range(1, 8):
            signal(self.along_z(s))
        signal(self.partner())

    def greeted(self):
        pl.semaphore_wait(pltpu.get_barrier_semaphore(), 23)


def exchange(place, solve, payload, keep, out, got, mine, sems, cover, alone):
    if alone:
        cover()
        for k in range(16):
            value, extra = solve(payload[k, :16, :], payload[k, 16:17, :], keep.at[k])
            out[k, :16, :] = value
            out[k, 16:17, :] = extra
        return
    chip = place.chip
    scatter, spread, swap_sems = sems[0:2], sems[2:4], sems[4:6]

    def outward(s):
        target = (chip + s) % 16
        return remote(payload.at[target], got.at[s], scatter, s, place.chip_peer(target))

    def start(s, carry):
        outward(s).start()
        return carry

    lax.fori_loop(1, 16, start, 0)
    cover()
    mine[0] = payload[chip]

    def add(s, carry):
        outward(s).wait_recv()
        mine[0] += got[s]
        return carry

    lax.fori_loop(1, 16, add, 0)
    swap = remote(mine.at[0], mine.at[1], swap_sems, 0, place.partner())
    swap.start()
    swap.wait_recv()
    value, extra = solve(mine[0, :16, :] + mine[1, :16, :], mine[0, 16:17, :] + mine[1, 16:17, :], keep.at[0])
    mine[2, :16, :] = value
    mine[2, 16:17, :] = extra

    def back(s):
        return remote(mine.at[2], out.at[chip], spread, s, place.chip_peer((chip + s) % 16))

    def arrival(s):
        return remote(mine.at[2], out.at[(chip + 16 - s) % 16], spread, s, place.chip_peer((chip + s) % 16))

    def start_back(s, carry):
        back(s).start()
        return carry

    lax.fori_loop(1, 16, start_back, 0)
    out[chip] = mine[2]

    def finish(s, carry):
        arrival(s).wait_recv()
        return carry

    lax.fori_loop(1, 16, finish, 0)

    def drain(s, carry):
        outward(s).wait_send()
        back(s).wait_send()
        return carry

    lax.fori_loop(1, 16, drain, 0)
    swap.wait_send()


class AxisSum:
    def __init__(self, chunk, me, peer, box, sems, at):
        self.chunk, self.me, self.box = chunk, me, box
        relay, raw, comb, held = (box.at[n] for n in range(4))
        self.held, self.relay_in, self.raw_in, self.comb_in = held, relay, raw, comb
        self.relay, self.raw, self.comb = [], [], []
        for i, s in enumerate((1, -1)):
            to = peer(s)
            near = (me + s + 4) % 4
            self.relay.append(remote(chunk((me + 2) % 4, i), relay.at[i], sems, at + 3 * i, to))
            self.raw.append(remote(chunk(near, 1 - i), raw.at[i], sems, at + 3 * i + 1, to))
            self.comb.append(remote(held.at[i], comb.at[i], sems, at + 3 * i + 2, to))

    def begin(self):
        for i in range(2):
            self.relay[i].start()
        for i in range(2):
            self.raw[i].start()

    def combine(self):
        for i, s in enumerate((1, -1)):
            near = (self.me + s + 4) % 4
            self.relay[i].wait_recv()
            for n in range(2):
                self.held[i, n] = self.chunk(near, i)[n] + self.relay_in[i, n]
            self.comb[i].start()

    def end(self, store):
        for i in range(2):
            self.comb[i].wait_recv()
            self.raw[1 - i].wait_recv()
            for n in range(2):
                store(2 * i + n, self.chunk(self.me, i)[n] + self.comb_in[i, n] + self.raw_in[1 - i, n])

    def drain(self):
        for one in self.relay + self.raw + self.comb:
            one.wait_send()


class OwnerSum:
    def __init__(self, place, grads, other, total, half, last, wide, thin, sems):
        self.place, self.grads, self.other, self.total = place, grads, other, total
        self.half, self.last = half, last
        core = place.core
        self.swaps = [
            remote(grads.at[1 - core, 4 * h : 4 * h + 4], other.at[4 * h : 4 * h + 4], sems, h, place.partner())
            for h in range(2)
        ]
        self.wide = [
            AxisSum(lambda d, n: total.at[2 * n : 2 * n + 2, d], place.x, place.along_x, wide.at[0], sems, 2),
            AxisSum(lambda d, n: total.at[4 + 2 * n : 6 + 2 * n, :, d], place.y, place.along_y, wide.at[1], sems, 8),
        ]
        self.thin = [
            AxisSum(lambda d, n: half.at[0, 2 * n : 2 * n + 2, d], place.y, place.along_y, thin.at[0], sems, 14),
            AxisSum(lambda d, n: half.at[1, 2 * n : 2 * n + 2, d], place.x, place.along_x, thin.at[1], sems, 20),
        ]
        self.final = [
            remote(last.at[0, (place.z + s) % 8], last.at[1, s], sems, 25 + s, place.along_z(s)) for s in range(1, 8)
        ]

    def swap(self):
        for one in self.swaps:
            one.start()

    def join(self):
        for h in range(2):
            self.swaps[h].wait_recv()

            def body(i, carry):
                self.total[4 * h + i] = self.grads[self.place.core, 4 * h + i] + self.other[4 * h + i]
                return carry

            lax.fori_loop(0, 4, body, 0)
            self.wide[h].begin()

    def combine_wide(self):
        for h in range(2):
            self.wide[h].combine()

    def turn(self):
        for h in range(2):

            def store(n, value):
                self.half[h, n] = value

            self.wide[h].end(store)
            self.thin[h].begin()

    def combine_thin(self):
        for h in range(2):
            self.thin[h].combine()

    def deepen(self):
        for h in range(2):

            def store(n, value):
                self.last[0, 4 * h + n] = value

            self.thin[h].end(store)
        for one in self.final:
            one.start()

    def result(self):
        value = self.last[0, self.place.z]
        for s in range(1, 8):
            self.final[s - 1].wait_recv()
            value = value + self.last[1, s]
        return value

    def drain(self):
        for one in self.swaps + self.final:
            one.wait_send()
        for one in self.wide + self.thin:
            one.drain()


EARLY, LATE = 32, 8


def slot_rows(core, slot, slots):
    return pl.ds(core * 128 * slots + slot, 128, stride=slots)


def pack_gains(gains):
    total = jnp.sum(gains[...], axis=0, keepdims=True)
    row = lax.broadcasted_iota(jnp.int32, (256, 1024), 0)
    own = (row & 127) * 2 + (row >> 7)
    channel = lax.broadcasted_iota(jnp.int32, (256, 1024), 1)
    spread = jnp.where((channel >> 2) == own, total, 0.0)
    channel = lax.broadcasted_iota(jnp.int32, (1024, 128), 0)
    lane = lax.broadcasted_iota(jnp.int32, (1024, 128), 1)
    pick = jnp.where((channel & 3) == lane, 1.0, 0.0).astype(BF16)
    return dot_parts(parts(spread, 3), [pick])


def kernel(
    span, scale, alone,
    x_in, og_in, a_in, b_in, c_in, gain, input_grad, sums, *scratch,
):
    (
        x, og, a, b, c, acc, padded, columns, h1, s1, h2, s2, gram, hsum, wide, payload, payload2, keep, whites,
        slopes, got, got2, mine, mine2, diagonal, diagonal2, row, white, dpre, dwhite, d, across, csum, gains, e,
        last, mid, top, early, late, early_other, late_other, early_total, late_total, early_half, late_half,
        early_last, late_last, early_wide, late_wide, early_thin, late_thin, grad_out, load_sems, *sems,
    ) = scratch
    place = None if alone else Place()
    loads = [
        pltpu.make_async_copy(source, target, load_sems.at[n])
        for n, (source, target) in enumerate(((a_in, a), (x_in, x), (b_in, b), (c_in, c), (og_in, og)))
    ]
    for one in loads:
        one.start()
    if not alone:
        place.greet()
    rows = x.shape[0]
    padded[:PAD, :] = jnp.zeros((PAD, 256), F32)
    padded[rows + PAD :, :] = jnp.zeros((PAD, 256), F32)

    loads[0].wait()
    loads[1].wait()
    acc[...] = dot(x[...], a[...])

    def first(t, carry):
        v = acc[tile_rows(t), :]
        s = 1.0 / (1.0 + jnp.exp(-v))
        s1[tile_rows(t), :] = s * (1.0 + v * (1.0 - s))
        h = (v * s).astype(BF16)
        h1[tile_rows(t), :] = h
        padded[pl.ds(t * TILE + PAD, TILE), :] = h.astype(F32)
        return carry

    lax.fori_loop(0, rows // TILE, first, 0)
    shifted_tiles(padded, columns, 1)
    loads[2].wait()
    acc[...] = dot(columns[...], b[...])

    def second(t, carry):
        v = acc[tile_rows(t), :]
        s = 1.0 / (1.0 + jnp.exp(-v))
        s2[tile_rows(t), :] = s * (1.0 + v * (1.0 - s))
        h2[tile_rows(t), :] = (v * s).astype(BF16)
        return carry

    lax.fori_loop(0, rows // TILE, second, 0)
    gram[...] = dot(h2[...], h2[...], ((0,), (0,)))
    loads[3].wait()
    wide[...] = dot_parts(parts(gram[...], 3), [c[...]])
    brow = dot_parts(parts(dot(jnp.ones((8, rows), BF16), h2[...]), 3), [c[...]])

    def squares(j):
        here = slice(j * 256, j * 256 + 256)
        return dot_parts([c[:, here]], parts(wide[:, here], 3), ((0,), (0,)))

    fill_payload(payload, squares, brow[:1])
    if not alone:
        place.greeted()

    def cover():
        hsum[...] = dot(h2[...], jnp.ones((rows, 128), BF16), ((0,), (0,)))
        loads[4].wait()

    exchange(
        place, lambda *args: solve_white(span, *args), payload, keep, whites, got, mine, sems[0:6], cover, alone
    )

    fill_diagonal(diagonal, whites)
    fill_row(row, whites)
    for j in range(4):
        here = slice(j * 256, j * 256 + 256)
        folded = dot_parts([c[:, here]], parts(diagonal[j], 2))
        high, low = parts(folded, 2)
        d[:, here] = high
        white[:, here] = dot(h2[...], high) + dot(h2[...], low)
    csum[...] = jnp.zeros_like(csum)
    gains[...] = jnp.zeros_like(gains)

    def slope(t, carry):
        for j in range(8):
            here = slice(j * 128, j * 128 + 128)
            w = white[tile_rows(t), here] - row[0:1, here]
            g = gain[0:1, here]
            v = x[tile_rows(t), here].astype(F32) + g * w
            s = 1.0 / (1.0 + jnp.exp(-v))
            u = og[tile_rows(t), here].astype(F32) * (s * (1.0 + v * (1.0 - s)))
            dpre[tile_rows(t), here] = u
            dw = g * u
            dwhite[tile_rows(t), here] = dw.astype(BF16)
            csum[:, here] += jnp.sum(dw.reshape(TILE // 8, 8, 128), axis=0)
            gains[:, here] += jnp.sum((u * w).reshape(TILE // 8, 8, 128), axis=0)
        return carry

    lax.fori_loop(0, rows // TILE, slope, 0)
    across[...] = dot(h2[...], dwhite[...], ((0,), (0,)))

    def squares2(j):
        here = slice(j * 256, j * 256 + 256)
        square = dot_parts([c[:, here]], parts(across[:, here], 2), ((0,), (0,)))
        return 0.5 * (square + square.T)

    fill_payload(payload2, squares2, jnp.sum(csum[...], axis=0, keepdims=True))

    def cover2():
        acc[...] = dot(dwhite[...], d[...], ((1,), (1,)))
        for j in range(4):
            here = slice(j * 256, j * 256 + 256)
            high, low = parts(across[:, here], 2)
            pieces = parts(diagonal[j], 2)
            value = dot_parts([high], pieces, ((1,), (1,))) + dot(low, pieces[0], ((1,), (1,)))
            for half in range(2):
                last[2 * j + half] = value[:, half * 128 : half * 128 + 128]

    exchange(
        place, lambda *args: solve_slope(span, *args), payload2, keep, slopes, got2, mine2, sems[6:12], cover2, alone
    )

    fill_diagonal(diagonal2, slopes)
    fill_row(row, slopes)
    for j in range(4):
        here = slice(j * 256, j * 256 + 256)
        e[:, here] = (dot_parts([c[:, here]], parts(diagonal2[j], 2)) * (1.0 / span)).astype(BF16)
    back = dot(e[...], c[...], ((1,), (1,))).astype(BF16)
    const = dot_parts(parts(jnp.broadcast_to(row[0:1, :], (8, 1024)), 2), [c[...]], ((1,), (1,)))
    acc[...] += dot(h2[...], back)

    def dmid2(t, carry):
        v = (acc[tile_rows(t), :] - const[0:1, :]) * s2[tile_rows(t), :]
        padded[pl.ds(t * TILE + PAD, TILE), :] = v.astype(BF16).astype(F32)
        return carry

    lax.fori_loop(0, rows // TILE, dmid2, 0)
    shifted_tiles(padded, columns, -1)
    for tap in range(9):
        here = slice(tap * 256, tap * 256 + 256)
        value = dot(h1[...], columns[:, here], ((0,), (0,)))
        for half in range(2):
            mid[half, here, :] = value[:, half * 128 : half * 128 + 128]
    grams = parts(gram[...], 2)
    for j in range(4):
        value = dot_parts(grams, [e[:, j * 256 : j * 256 + 256]])
        for half in range(2):
            n = 2 * j + half
            here = slice(n * 128, n * 128 + 128)
            last[n] = last[n] + value[:, half * 128 : half * 128 + 128] - hsum[...] * row[0:1, here]
    value = pack_gains(gains)
    for core in range(2):
        for j in range(8):
            early[slot_rows(core, j, EARLY), :] = last[j, pl.ds(core, 128, stride=2), :]
        for half in range(2):
            for q in range(9):
                early[slot_rows(core, 8 + 2 * q + half, EARLY), :] = mid[half, pl.ds(q + 9 * core, 128, stride=18), :]
        early[slot_rows(core, 26, EARLY), :] = value[core * 128 : core * 128 + 128]
        for slot in range(27, 32):
            early[slot_rows(core, slot, EARLY), :] = jnp.zeros((128, 128), F32)
    if not alone:
        early_sum = OwnerSum(
            place, early.reshape(2, 8, 4, 4, EARLY, 128), early_other, early_total, early_half, early_last,
            early_wide, early_thin, sems[12:14],
        )
        late_sum = OwnerSum(
            place, late.reshape(2, 8, 4, 4, LATE, 128), late_other, late_total, late_half, late_last, late_wide,
            late_thin, sems[14:16],
        )
        early_sum.swap()
    for tap in range(9):
        here = slice(tap * 256, tap * 256 + 256)
        term = dot(columns[:, here], b[here, :], ((1,), (1,)))
        if tap == 0:
            acc[...] = term
        else:
            acc[...] += term
    if not alone:
        early_sum.join()

    def dmid1(t, carry):
        dwhite[tile_rows(t), :256] = (acc[tile_rows(t), :] * s1[tile_rows(t), :]).astype(BF16)
        return carry

    lax.fori_loop(0, rows // TILE, dmid1, 0)
    value = dot(x[...], dwhite[:, :256], ((0,), (0,)))
    for half in range(2):
        top[half] = value[:, half * 128 : half * 128 + 128]
    for core in range(2):
        for half in range(2):
            for q in range(4):
                late[slot_rows(core, 2 * q + half, LATE), :] = top[half, pl.ds(q + 4 * core, 128, stride=8), :]
    if not alone:
        late_sum.swap()
        early_sum.combine_wide()
    for j in range(4):
        here = slice(j * 256, j * 256 + 256)
        grad_out[:, here] = (dot(dwhite[:, :256], a[here, :], ((1,), (1,))) + dpre[:, here]).astype(BF16)
    store = pltpu.make_async_copy(grad_out, input_grad, load_sems.at[5])
    store.start()
    if alone:
        sums[:, :32, :] = early[...].reshape(256, 32, 128)
        sums[:, 32:, :] = late[...].reshape(256, 8, 128)
    else:
        late_sum.join()
        early_sum.turn()
        late_sum.combine_wide()
        early_sum.combine_thin()
        late_sum.turn()
        early_sum.deepen()
        late_sum.combine_thin()
        late_sum.deepen()
        sums[:EARLY, :] = early_sum.result() * scale
        sums[EARLY:, :] = late_sum.result() * scale
        early_sum.drain()
        late_sum.drain()
    store.wait()


VM = pl.BlockSpec(memory_space=pltpu.VMEM)
ANY = pl.BlockSpec(memory_space=pl.ANY)


def shape(dims, kind=F32):
    return jax.ShapeDtypeStruct(dims, kind)


def block_step(inputs, out_grad, conv_first, conv_middle, conv_last, gain, span, scale, alone=False):
    rows = inputs.shape[0]

    def body(*refs):
        kernel(span, scale, alone, *refs)

    def vmem(*dims, kind=F32):
        return pltpu.VMEM(dims, kind)

    dma = pltpu.SemaphoreType.DMA
    grown = [vmem(8, 4, 4, size, 128) for size in (EARLY, LATE)]
    scratch = [
        vmem(rows, 1024, kind=BF16), vmem(rows, 1024, kind=BF16), vmem(1024, 256, kind=BF16),
        vmem(2304, 256, kind=BF16), vmem(256, 1024, kind=BF16),
        vmem(rows, 256), vmem(rows + 2 * PAD, 256), vmem(rows, 2304, kind=BF16),
        vmem(rows, 256, kind=BF16), vmem(rows, 256), vmem(rows, 256, kind=BF16), vmem(rows, 256),
        vmem(256, 256), vmem(256, 128), vmem(256, 1024),
        vmem(16, 17, 128), vmem(16, 17, 128), vmem(16 if alone else 1, 136, 64),
        vmem(16, 17, 128), vmem(16, 17, 128), vmem(16, 17, 128), vmem(16, 17, 128),
        vmem(3, 17, 128), vmem(3, 17, 128),
        vmem(4, 256, 256), vmem(4, 256, 256), vmem(8, 1024),
        vmem(rows, 1024), vmem(rows, 1024), vmem(rows, 1024, kind=BF16), vmem(256, 1024, kind=BF16),
        vmem(256, 1024), vmem(8, 1024), vmem(8, 1024), vmem(256, 1024, kind=BF16),
        vmem(8, 256, 128), vmem(2, 2304, 128), vmem(2, 1024, 128),
        vmem(256 * EARLY, 128), vmem(256 * LATE, 128), *grown, *grown,
        vmem(2, 4, 4, EARLY, 128), vmem(2, 4, 4, LATE, 128),
        vmem(2, 8, EARLY, 128), vmem(2, 8, LATE, 128),
        vmem(2, 4, 2, 2, 4, EARLY, 128), vmem(2, 4, 2, 2, 4, LATE, 128),
        vmem(2, 4, 2, 2, EARLY, 128), vmem(2, 4, 2, 2, LATE, 128),
        vmem(rows, 1024, kind=BF16),
        dma((6,)), *([dma((16,))] * 4 + [dma((1,))] * 2) * 2, *[dma((33,))] * 4,
    ]
    params = {} if alone else dict(collective_id=0, has_side_effects=True)
    return pl.pallas_call(
        body,
        out_shape=(shape((rows, 1024), BF16), shape((256, 40, 128) if alone else (EARLY + LATE, 128))),
        in_specs=[ANY] * 5 + [VM],
        out_specs=(ANY, VM),
        scratch_shapes=scratch,
        compiler_params=pltpu.CompilerParams(vmem_limit_bytes=67043328, **params),
        name="block_step",
    )(inputs, out_grad, conv_first, conv_middle, conv_last, gain.reshape(1, -1))


def shards(inputs, out_grad, conv_first, conv_middle, conv_last, gain):
    ghosts, groups = lax.axis_size("ghost"), lax.axis_size("group")
    span = float(inputs.shape[0] * ghosts)
    input_grad, sums = block_step(
        inputs, out_grad, conv_first, conv_middle, conv_last, gain, span, (span * groups) ** (-0.5)
    )
    return (
        input_grad, sums[32:40].reshape(-1), sums[8:26].reshape(-1), sums[0:8].reshape(-1), sums[26, :4]
    )


def newton(n, size):
    row = lax.broadcasted_iota(jnp.int32, (size, size), 0)
    lane = lax.broadcasted_iota(jnp.int32, (size, size), 1)
    project = jnp.where(row == lane, 1.5, 0.0) - 0.5 * n
    for sweep in range(NEWTON - 1):
        squared = dot_high(project, project)
        project = 1.5 * project - 0.5 * dot_high(squared, dot_high(project, n))
    return project


def trace_of(block, size=64):
    row = lax.broadcasted_iota(jnp.int32, (size, size), 0)
    lane = lax.broadcasted_iota(jnp.int32, (size, size), 1)
    return jnp.sum(jnp.where(row == lane, block, 0.0))


def solution(mesh):
    rows = P(("group", "ghost"))
    return jax.shard_map(
        shards,
        mesh=mesh,
        in_specs=(P(("group", "ghost"), None), P(("group", "ghost"), None), P(), P(), P(), P()),
        out_specs=(P(("group", "ghost"), None), rows, rows, rows, rows),
        check_vma=False,
    )
```

profile of v0, /device:TPU:2, one launch (start us, length us, event | category | flops | bytes accessed | tf_op | source)
XLA Modules:
  0.0 97.0 jit_solution(14999754569525845249)
XLA Ops:
  0.6 89.8 %block_step.1 = (bf16[784,1024]{1,0:T(8,128)(2,1)}, f32[40,128]{1,0:T(8,128)}) custom-call(bf16[784,1024]{1,0:T(8,128)(2,1)} %refs_0_.1, bf16[784,1024]{1,0:T(8,128)(2,1)} %refs_1_.1, bf16[1024,256]{1,0:T(8,128)(2,1)} %refs_2_.1, bf16[2304,256]{1,0:T(8,128)(2,1)} %refs_3_.1, bf16[256,1024]{1,0:T(8,128)(2,1)} %refs_4_.1, f32[1,1024]{1,0:T(1,128)} %bitcast.9), custom_call_target="tpu_custom_call" | custom-call | tf_op jit(solution)/shard_map/block_step/pallas_call | solution.py:698
  90.5 1.2 %slice_bitcast_fusion.3 = f32[4]{0:T(128)} fusion(f32[40,128]{1,0:T(8,128)} %get-tuple-element.8), kind=kLoop, calls=%fused_computation.3 | loop fusion | bytes 32 | tf_op jit(solution)/shard_map/squeeze | solution.py:716
  91.7 1.3 %slice_bitcast_fusion.1 = (f32[1024]{0:T(1024)}, f32[1024]{0:T(1024)}) fusion(f32[40,128]{1,0:T(8,128)} %get-tuple-element.8), kind=kLoop, calls=%fused_computation.1 | loop fusion | bytes 16384 | tf_op jit(solution)/shard_map/reshape | solution.py:716
  93.0 1.3 %slice_bitcast_fusion = f32[2304]{0:T(1024)} fusion(f32[40,128]{1,0:T(8,128)} %get-tuple-element.8), kind=kLoop, calls=%fused_computation | loop fusion | bytes 18432 | tf_op jit(solution)/shard_map/reshape | solution.py:716
  94.3 2.7 %copy.12 = bf16[784,1024]{1,0:T(8,128)(2,1)} copy(bf16[784,1024]{1,0:T(8,128)(2,1)} %get-tuple-element.16) | data formatting | bytes 3211264
where the time goes:
time: 97.3 us; the launch traced here: 97 us
  Pallas kernels  89.8 us (92%)
  local copies, waits for them, and re-layouts  6.48 us (7%)
    pallas_call x1, Pallas kernels, block_step(): pl.pallas_call(body, out_shape=(shape((rows, 1024), BF16), shape((256, 40...  89.8 us
    unnamed x1, local copies, waits for them, and re-layouts  2.69 us

commit v1 on v0

--- a/solution.py
+++ b/solution.py
@@ -194,6 +194,22 @@
     return packed_of(sym, line[:1] * (1.0 / span))
 
 
+def newton(n, size):
+    row = lax.broadcasted_iota(jnp.int32, (size, size), 0)
+    lane = lax.broadcasted_iota(jnp.int32, (size, size), 1)
+    project = jnp.where(row == lane, 1.5, 0.0) - 0.5 * n
+    for sweep in range(NEWTON - 1):
+        squared = dot_high(project, project)
+        project = 1.5 * project - 0.5 * dot_high(squared, dot_high(project, n))
+    return project
+
+
+def trace_of(block, size=64):
+    row = lax.broadcasted_iota(jnp.int32, (size, size), 0)
+    lane = lax.broadcasted_iota(jnp.int32, (size, size), 1)
+    return jnp.sum(jnp.where(row == lane, block, 0.0))
+
+
 def remote(source, target, sems, at, peer):
     send, recv = sems
     return pltpu.make_async_remote_copy(
@@ -342,12 +358,17 @@
 
 
 class OwnerSum:
-    def __init__(self, place, grads, other, total, half, last, wide, thin, sems):
-        self.place, self.grads, self.other, self.total = place, grads, other, total
+    def __init__(self, place, grads, other, total, half, last, wide, thin, *sems):
+        self.place, self.other, self.total = place, other, total
         self.half, self.last = half, last
-        core = place.core
+        used, slots = other.shape[3], grads.shape[0] // 256
+        grads = grads.reshape(2, 8, 4, 4, slots, 128)
+        self.own = lambda z: grads[place.core, z, :, :, :used, :]
         self.swaps = [
-            remote(grads.at[1 - core, 4 * h : 4 * h + 4], other.at[4 * h : 4 * h + 4], sems, h, place.partner())
+            remote(
+                grads.at[1 - place.core, 4 * h : 4 * h + 4, :, :, :used, :], other.at[4 * h : 4 * h + 4], sems, h,
+                place.partner(),
+            )
             for h in range(2)
         ]
         self.wide = [
@@ -371,7 +392,7 @@
             self.swaps[h].wait_recv()
 
             def body(i, carry):
-                self.total[4 * h + i] = self.grads[self.place.core, 4 * h + i] + self.other[4 * h + i]
+                self.total[4 * h + i] = self.own(4 * h + i) + self.other[4 * h + i]
                 return carry
 
             lax.fori_loop(0, 4, body, 0)
@@ -418,11 +439,21 @@
             one.drain()
 
 
-EARLY, LATE = 32, 8
-
-
 def slot_rows(core, slot, slots):
     return pl.ds(core * 128 * slots + slot, 128, stride=slots)
+
+
+USED = (8, 19, 8)
+SLOTS = (8, 24, 8)
+
+
+def store_slots(target, source, count, step, at):
+    slots = target.shape[0] // 256
+    for core in range(2):
+        for n in range(source.shape[0]):
+            for q in range(count):
+                rows = pl.ds(q + step * core, 128, stride=2 * step)
+                target[slot_rows(core, at + n + q * source.shape[0], slots), :] = source[n, rows, :]
 
 
 def pack_gains(gains):
@@ -444,9 +475,10 @@
     (
         x, og, a, b, c, acc, padded, columns, h1, s1, h2, s2, gram, hsum, wide, payload, payload2, keep, whites,
         slopes, got, got2, mine, mine2, diagonal, diagonal2, row, white, dpre, dwhite, d, across, csum, gains, e,
-        last, mid, top, early, late, early_other, late_other, early_total, late_total, early_half, late_half,
-        early_last, late_last, early_wide, late_wide, early_thin, late_thin, grad_out, load_sems, *sems,
+        last, mid, top, grad_out, load_sems, *rest,
     ) = scratch
+    sems, rest = rest[:12], rest[12:]
+    groups = [rest[n :: 3] for n in range(3)]
     place = None if alone else Place()
     loads = [
         pltpu.make_async_copy(source, target, load_sems.at[n])
@@ -562,22 +594,6 @@
     for j in range(4):
         here = slice(j * 256, j * 256 + 256)
         e[:, here] = (dot_parts([c[:, here]], parts(diagonal2[j], 2)) * (1.0 / span)).astype(BF16)
-    back = dot(e[...], c[...], ((1,), (1,))).astype(BF16)
-    const = dot_parts(parts(jnp.broadcast_to(row[0:1, :], (8, 1024)), 2), [c[...]], ((1,), (1,)))
-    acc[...] += dot(h2[...], back)
-
-    def dmid2(t, carry):
-        v = (acc[tile_rows(t), :] - const[0:1, :]) * s2[tile_rows(t), :]
-        padded[pl.ds(t * TILE + PAD, TILE), :] = v.astype(BF16).astype(F32)
-        return carry
-
-    lax.fori_loop(0, rows // TILE, dmid2, 0)
-    shifted_tiles(padded, columns, -1)
-    for tap in range(9):
-        here = slice(tap * 256, tap * 256 + 256)
-        value = dot(h1[...], columns[:, here], ((0,), (0,)))
-        for half in range(2):
-            mid[half, here, :] = value[:, half * 128 : half * 128 + 128]
     grams = parts(gram[...], 2)
     for j in range(4):
         value = dot_parts(grams, [e[:, j * 256 : j * 256 + 256]])
@@ -585,26 +601,40 @@
             n = 2 * j + half
             here = slice(n * 128, n * 128 + 128)
             last[n] = last[n] + value[:, half * 128 : half * 128 + 128] - hsum[...] * row[0:1, here]
+    store_slots(groups[0][0], last, 1, 1, 0)
+    if alone:
+        one = two = three = None
+    else:
+        one, two, three = (OwnerSum(place, *group) for group in groups)
+        one.swap()
+    back = dot(e[...], c[...], ((1,), (1,))).astype(BF16)
+    const = dot_parts(parts(jnp.broadcast_to(row[0:1, :], (8, 1024)), 2), [c[...]], ((1,), (1,)))
+    acc[...] += dot(h2[...], back)
+
+    def dmid2(t, carry):
+        v = (acc[tile_rows(t), :] - const[0:1, :]) * s2[tile_rows(t), :]
+        padded[pl.ds(t * TILE + PAD, TILE), :] = v.astype(BF16).astype(F32)
+        return carry
+
+    lax.fori_loop(0, rows // TILE, dmid2, 0)
+    if not alone:
+        one.join()
+    shifted_tiles(padded, columns, -1)
+    if not alone:
+        one.combine_wide()
+    for tap in range(9):
+        here = slice(tap * 256, tap * 256 + 256)
+        value = dot(h1[...], columns[:, here], ((0,), (0,)))
+        for half in range(2):
+            mid[half, here, :] = value[:, half * 128 : half * 128 + 128]
+    target = groups[1][0]
+    store_slots(target, mid, 9, 9, 0)
     value = pack_gains(gains)
     for core in range(2):
-        for j in range(8):
-            early[slot_rows(core, j, EARLY), :] = last[j, pl.ds(core, 128, stride=2), :]
-        for half in range(2):
-            for q in range(9):
-                early[slot_rows(core, 8 + 2 * q + half, EARLY), :] = mid[half, pl.ds(q + 9 * core, 128, stride=18), :]
-        early[slot_rows(core, 26, EARLY), :] = value[core * 128 : core * 128 + 128]
-        for slot in range(27, 32):
-            early[slot_rows(core, slot, EARLY), :] = jnp.zeros((128, 128), F32)
+        target[slot_rows(core, 18, SLOTS[1]), :] = value[core * 128 : core * 128 + 128]
     if not alone:
-        early_sum = OwnerSum(
-            place, early.reshape(2, 8, 4, 4, EARLY, 128), early_other, early_total, early_half, early_last,
-            early_wide, early_thin, sems[12:14],
-        )
-        late_sum = OwnerSum(
-            place, late.reshape(2, 8, 4, 4, LATE, 128), late_other, late_total, late_half, late_last, late_wide,
-            late_thin, sems[14:16],
-        )
-        early_sum.swap()
+        two.swap()
+        one.turn()
     for tap in range(9):
         here = slice(tap * 256, tap * 256 + 256)
         term = dot(columns[:, here], b[here, :], ((1,), (1,)))
@@ -612,8 +642,10 @@
             acc[...] = term
         else:
             acc[...] += term
+        if tap == 4 and not alone:
+            one.combine_thin()
     if not alone:
-        early_sum.join()
+        two.join()
 
     def dmid1(t, carry):
         dwhite[tile_rows(t), :256] = (acc[tile_rows(t), :] * s1[tile_rows(t), :]).astype(BF16)
@@ -623,34 +655,36 @@
     value = dot(x[...], dwhite[:, :256], ((0,), (0,)))
     for half in range(2):
         top[half] = value[:, half * 128 : half * 128 + 128]
-    for core in range(2):
-        for half in range(2):
-            for q in range(4):
-                late[slot_rows(core, 2 * q + half, LATE), :] = top[half, pl.ds(q + 4 * core, 128, stride=8), :]
+    store_slots(groups[2][0], top, 4, 4, 0)
     if not alone:
-        late_sum.swap()
-        early_sum.combine_wide()
+        three.swap()
+        two.combine_wide()
+        one.deepen()
     for j in range(4):
         here = slice(j * 256, j * 256 + 256)
         grad_out[:, here] = (dot(dwhite[:, :256], a[here, :], ((1,), (1,))) + dpre[:, here]).astype(BF16)
+        if j == 1 and not alone:
+            three.join()
     store = pltpu.make_async_copy(grad_out, input_grad, load_sems.at[5])
     store.start()
     if alone:
-        sums[:, :32, :] = early[...].reshape(256, 32, 128)
-        sums[:, 32:, :] = late[...].reshape(256, 8, 128)
+        sums[:, :8, :] = groups[0][0][...].reshape(256, 8, 128)
+        sums[:, 8:32, :] = groups[1][0][...].reshape(256, 24, 128)
+        sums[:, 32:, :] = groups[2][0][...].reshape(256, 8, 128)
     else:
-        late_sum.join()
-        early_sum.turn()
-        late_sum.combine_wide()
-        early_sum.combine_thin()
-        late_sum.turn()
-        early_sum.deepen()
-        late_sum.combine_thin()
-        late_sum.deepen()
-        sums[:EARLY, :] = early_sum.result() * scale
-        sums[EARLY:, :] = late_sum.result() * scale
-        early_sum.drain()
-        late_sum.drain()
+        two.turn()
+        three.combine_wide()
+        two.combine_thin()
+        three.turn()
+        two.deepen()
+        three.combine_thin()
+        sums[0:8, :] = one.result() * scale
+        three.deepen()
+        sums[8:27, :] = two.result() * scale
+        sums[32:40, :] = three.result() * scale
+        one.drain()
+        two.drain()
+        three.drain()
     store.wait()
 
 
@@ -672,7 +706,6 @@
         return pltpu.VMEM(dims, kind)
 
     dma = pltpu.SemaphoreType.DMA
-    grown = [vmem(8, 4, 4, size, 128) for size in (EARLY, LATE)]
     scratch = [
         vmem(rows, 1024, kind=BF16), vmem(rows, 1024, kind=BF16), vmem(1024, 256, kind=BF16),
         vmem(2304, 256, kind=BF16), vmem(256, 1024, kind=BF16),
@@ -686,18 +719,17 @@
         vmem(rows, 1024), vmem(rows, 1024), vmem(rows, 1024, kind=BF16), vmem(256, 1024, kind=BF16),
         vmem(256, 1024), vmem(8, 1024), vmem(8, 1024), vmem(256, 1024, kind=BF16),
         vmem(8, 256, 128), vmem(2, 2304, 128), vmem(2, 1024, 128),
-        vmem(256 * EARLY, 128), vmem(256 * LATE, 128), *grown, *grown,
-        vmem(2, 4, 4, EARLY, 128), vmem(2, 4, 4, LATE, 128),
-        vmem(2, 8, EARLY, 128), vmem(2, 8, LATE, 128),
-        vmem(2, 4, 2, 2, 4, EARLY, 128), vmem(2, 4, 2, 2, 4, LATE, 128),
-        vmem(2, 4, 2, 2, EARLY, 128), vmem(2, 4, 2, 2, LATE, 128),
-        vmem(rows, 1024, kind=BF16),
-        dma((6,)), *([dma((16,))] * 4 + [dma((1,))] * 2) * 2, *[dma((33,))] * 4,
+        vmem(rows, 1024, kind=BF16), dma((6,)), *([dma((16,))] * 4 + [dma((1,))] * 2) * 2,
+        *(vmem(256 * size, 128) for size in SLOTS),
+        *(vmem(8, 4, 4, size, 128) for size in USED), *(vmem(8, 4, 4, size, 128) for size in USED),
+        *(vmem(2, 4, 4, size, 128) for size in USED), *(vmem(2, 8, size, 128) for size in USED),
+        *(vmem(2, 4, 2, 2, 4, size, 128) for size in USED), *(vmem(2, 4, 2, 2, size, 128) for size in USED),
+        *[dma((33,))] * 6,
     ]
     params = {} if alone else dict(collective_id=0, has_side_effects=True)
     return pl.pallas_call(
         body,
-        out_shape=(shape((rows, 1024), BF16), shape((256, 40, 128) if alone else (EARLY + LATE, 128))),
+        out_shape=(shape((rows, 1024), BF16), shape((256, 40, 128) if alone else (40, 128))),
         in_specs=[ANY] * 5 + [VM],
         out_specs=(ANY, VM),
         scratch_shapes=scratch,
@@ -706,31 +738,54 @@
     )(inputs, out_grad, conv_first, conv_middle, conv_last, gain.reshape(1, -1))
 
 
+def finish_kernel(source, sums, target, first, middle, last, gain, buffer, arrive, leave):
+    count = buffer.shape[0]
+    size = source.shape[0] // count
+
+    def copies(n):
+        rows = pl.ds(n * size, size)
+        return (
+            pltpu.make_async_copy(source.at[rows], buffer.at[n], arrive.at[n]),
+            pltpu.make_async_copy(buffer.at[n], target.at[rows], leave.at[n]),
+        )
+
+    for n in range(count):
+        copies(n)[0].start()
+    last[...] = sums[0:8, :]
+    middle[...] = sums[8:26, :]
+    gain[...] = sums[26:27, :4]
+    first[...] = sums[32:40, :]
+    for n in range(count):
+        copies(n)[0].wait()
+        copies(n)[1].start()
+    for n in range(count):
+        copies(n)[1].wait()
+
+
+def finish(input_grad, sums):
+    rows, width = input_grad.shape
+    count = 7
+    dma = pltpu.SemaphoreType.DMA
+    return pl.pallas_call(
+        finish_kernel,
+        out_shape=(
+            shape((rows, width), BF16), shape((8, 128)), shape((18, 128)), shape((8, 128)), shape((1, 4))
+        ),
+        in_specs=[ANY, VM],
+        out_specs=(ANY, VM, VM, VM, VM),
+        scratch_shapes=[pltpu.VMEM((count, rows // count, width), BF16), dma((count,)), dma((count,))],
+        name="finish",
+    )(input_grad, sums)
+
+
 def shards(inputs, out_grad, conv_first, conv_middle, conv_last, gain):
     ghosts, groups = lax.axis_size("ghost"), lax.axis_size("group")
     span = float(inputs.shape[0] * ghosts)
     input_grad, sums = block_step(
         inputs, out_grad, conv_first, conv_middle, conv_last, gain, span, (span * groups) ** (-0.5)
     )
-    return (
-        input_grad, sums[32:40].reshape(-1), sums[8:26].reshape(-1), sums[0:8].reshape(-1), sums[26, :4]
-    )
-
-
-def newton(n, size):
-    row = lax.broadcasted_iota(jnp.int32, (size, size), 0)
-    lane = lax.broadcasted_iota(jnp.int32, (size, size), 1)
-    project = jnp.where(row == lane, 1.5, 0.0) - 0.5 * n
-    for sweep in range(NEWTON - 1):
-        squared = dot_high(project, project)
-        project = 1.5 * project - 0.5 * dot_high(squared, dot_high(project, n))
-    return project
-
-
-def trace_of(block, size=64):
-    row = lax.broadcasted_iota(jnp.int32, (size, size), 0)
-    lane = lax.broadcasted_iota(jnp.int32, (size, size), 1)
-    return jnp.sum(jnp.where(row == lane, block, 0.0))
+    input_grad, *grads = finish(input_grad, sums)
+    return (input_grad, *(grad.reshape(-1) for grad in grads))
 
 
 def solution(mesh):

time: 97.3 us -> 95.1 us (0.977)
  local copies, waits for them, and re-layouts: 6.48 us -> 0 us
  Pallas kernels: 89.8 us -> 94.1 us
    pallas_call x0 -> x1, Pallas kernels: none -> 3.65 us  [finish(): pl.pallas_call(finish_kernel, out_shape=(shape((rows, width), BF16), shap...]
    unnamed x1 -> x0, local copies, waits for them, and re-layouts: 2.69 us -> none
    reshape x2 -> x0, local copies, waits for them, and re-layouts: 2.59 us -> none  [the longest x1 1.31 us: shards(): sums[8:26].reshape(-1)]
    squeeze x1 -> x0, local copies, waits for them, and re-layouts: 1.2 us -> none  [shards(): sums[26, :4]]
where the time goes in v1:
time: 95.1 us; the launch traced here: 94.9 us
  Pallas kernels  94.1 us (99%)
    pallas_call x1, Pallas kernels, block_step(): pl.pallas_call(body, out_shape=(shape((rows, 1024), BF16), shape((256, 40...  90.5 us
    pallas_call x1, Pallas kernels, finish(): pl.pallas_call(finish_kernel, out_shape=(shape((rows, width), BF16), shap...  3.65 us

profile of v1, /device:TPU:2, one launch (start us, length us, event | category | flops | bytes accessed | tf_op | source)
XLA Modules:
  0.0 94.9 jit_solution(1233522526909736884)
XLA Ops:
  0.6 90.5 %block_step.1 = (bf16[784,1024]{1,0:T(8,128)(2,1)}, f32[40,128]{1,0:T(8,128)}) custom-call(bf16[784,1024]{1,0:T(8,128)(2,1)} %refs_0_.1, bf16[784,1024]{1,0:T(8,128)(2,1)} %refs_1_.1, bf16[1024,256]{1,0:T(8,128)(2,1)} %refs_2_.1, bf16[2304,256]{1,0:T(8,128)(2,1)} %refs_3_.1, bf16[256,1024]{1,0:T(8,128)(2,1)} %refs_4_.1, f32[1,1024]{1,0:T(1,128)} %bitcast.5), custom_call_target="tpu_custom_call" | custom-call | tf_op jit(solution)/shard_map/block_step/pallas_call | solution.py:730
  91.1 3.6 %finish.1 = (bf16[784,1024]{1,0:T(8,128)(2,1)}, f32[8,128]{1,0:T(8,128)}, f32[18,128]{1,0:T(8,128)}, f32[8,128]{1,0:T(8,128)}, f32[1,4]{1,0:T(1,128)}) custom-call(bf16[784,1024]{1,0:T(8,128)(2,1)} %get-tuple-element.12.source, f32[40,128]{1,0:T(8,128)} %get-tuple-element.13.sums), custom_call_target="tpu_custom_call" | custom-call | tf_op jit(solution)/shard_map/finish/pallas_call | solution.py:769

commit v2 on v1

--- a/solution.py
+++ b/solution.py
@@ -44,16 +44,25 @@
     )
 
 
+def sigmoid(v):
+    return 0.5 + 0.5 * jnp.tanh(0.5 * v)
+
+
 def tile_rows(t):
     return pl.ds(pl.multiple_of(t * TILE, TILE), TILE)
 
 
 def edges(t):
-    row = lax.broadcasted_iota(jnp.int32, (TILE, 256), 0).astype(F32) + float(t * TILE)
+    row = lax.broadcasted_iota(jnp.int32, (TILE, 128), 0).astype(F32) + float(t * TILE)
     line = jnp.floor((row + 0.5) * (1.0 / SIDE))
     column = row - line * SIDE
     image = jnp.floor((line + 0.5) * (1.0 / SIDE))
     return line - image * SIDE, column
+
+
+def store_padded(padded, t, value):
+    for half in range(2):
+        padded[half, pl.ds(t * TILE + PAD, TILE), :] = value[:, half * 128 : half * 128 + 128]
 
 
 def shifted_tiles(padded, columns, sign):
@@ -63,16 +72,18 @@
         for tap in range(9):
             dr, dc = sign * (tap // 3 - 1), sign * (tap % 3 - 1)
             start = t * TILE + PAD + dr * SIDE + dc
-            value = padded[start : start + TILE, :]
             keep = None
             if dr:
                 keep = line > 0.5 if dr < 0 else line < SIDE - 1.5
             if dc:
                 side = column > 0.5 if dc < 0 else column < SIDE - 1.5
                 keep = side if keep is None else keep & side
-            if keep is not None:
-                value = jnp.where(keep, value, 0.0)
-            columns[at, tap * 256 : tap * 256 + 256] = value.astype(BF16)
+            for half in range(2):
+                value = padded[half, start : start + TILE, :]
+                if keep is not None:
+                    value = jnp.where(keep, value, 0.0)
+                lanes = tap * 256 + half * 128
+                columns[at, lanes : lanes + 128] = value.astype(BF16)
 
 
 def lanes_of(rows, right):
@@ -475,7 +486,7 @@
     (
         x, og, a, b, c, acc, padded, columns, h1, s1, h2, s2, gram, hsum, wide, payload, payload2, keep, whites,
         slopes, got, got2, mine, mine2, diagonal, diagonal2, row, white, dpre, dwhite, d, across, csum, gains, e,
-        last, mid, top, grad_out, load_sems, *rest,
+        last, mid, top, h1t, h2t, xt, at, bt, ct, grad_out, load_sems, *rest,
     ) = scratch
     sems, rest = rest[:12], rest[12:]
     groups = [rest[n :: 3] for n in range(3)]
@@ -489,8 +500,8 @@
     if not alone:
         place.greet()
     rows = x.shape[0]
-    padded[:PAD, :] = jnp.zeros((PAD, 256), F32)
-    padded[rows + PAD :, :] = jnp.zeros((PAD, 256), F32)
+    padded[:, :PAD, :] = jnp.zeros((2, PAD, 128), F32)
+    padded[:, rows + PAD :, :] = jnp.zeros((2, PAD, 128), F32)
 
     loads[0].wait()
     loads[1].wait()
@@ -498,11 +509,11 @@
 
     def first(t, carry):
         v = acc[tile_rows(t), :]
-        s = 1.0 / (1.0 + jnp.exp(-v))
+        s = sigmoid(v)
         s1[tile_rows(t), :] = s * (1.0 + v * (1.0 - s))
         h = (v * s).astype(BF16)
         h1[tile_rows(t), :] = h
-        padded[pl.ds(t * TILE + PAD, TILE), :] = h.astype(F32)
+        store_padded(padded, t, h.astype(F32))
         return carry
 
     lax.fori_loop(0, rows // TILE, first, 0)
@@ -512,13 +523,14 @@
 
     def second(t, carry):
         v = acc[tile_rows(t), :]
-        s = 1.0 / (1.0 + jnp.exp(-v))
+        s = sigmoid(v)
         s2[tile_rows(t), :] = s * (1.0 + v * (1.0 - s))
         h2[tile_rows(t), :] = (v * s).astype(BF16)
         return carry
 
     lax.fori_loop(0, rows // TILE, second, 0)
-    gram[...] = dot(h2[...], h2[...], ((0,), (0,)))
+    h2t[...] = h2[...].T
+    gram[...] = dot(h2t[...], h2[...])
     loads[3].wait()
     wide[...] = dot_parts(parts(gram[...], 3), [c[...]])
     brow = dot_parts(parts(dot(jnp.ones((8, rows), BF16), h2[...]), 3), [c[...]])
@@ -532,7 +544,16 @@
         place.greeted()
 
     def cover():
-        hsum[...] = dot(h2[...], jnp.ones((rows, 128), BF16), ((0,), (0,)))
+        hsum[...] = dot(h2t[...], jnp.ones((rows, 128), BF16))
+        h1t[...] = h1[...].T
+        for n in range(4):
+            here = slice(n * 256, n * 256 + 256)
+            xt[here, :] = x[:, here].T
+            at[:, here] = a[here, :].T
+            ct[here, :] = c[:, here].T
+        for tap in range(9):
+            here = slice(tap * 256, tap * 256 + 256)
+            bt[here, :] = b[here, :].T
         loads[4].wait()
 
     exchange(
@@ -556,7 +577,7 @@
             w = white[tile_rows(t), here] - row[0:1, here]
             g = gain[0:1, here]
             v = x[tile_rows(t), here].astype(F32) + g * w
-            s = 1.0 / (1.0 + jnp.exp(-v))
+            s = sigmoid(v)
             u = og[tile_rows(t), here].astype(F32) * (s * (1.0 + v * (1.0 - s)))
             dpre[tile_rows(t), here] = u
             dw = g * u
@@ -566,7 +587,7 @@
         return carry
 
     lax.fori_loop(0, rows // TILE, slope, 0)
-    across[...] = dot(h2[...], dwhite[...], ((0,), (0,)))
+    across[...] = dot(h2t[...], dwhite[...])
 
     def squares2(j):
         here = slice(j * 256, j * 256 + 256)
@@ -584,6 +605,9 @@
             value = dot_parts([high], pieces, ((1,), (1,))) + dot(low, pieces[0], ((1,), (1,)))
             for half in range(2):
                 last[2 * j + half] = value[:, half * 128 : half * 128 + 128]
+        value = pack_gains(gains)
+        for core in range(2):
+            groups[1][0][slot_rows(core, 18, SLOTS[1]), :] = value[core * 128 : core * 128 + 128]
 
     exchange(
         place, lambda *args: solve_slope(span, *args), payload2, keep, slopes, got2, mine2, sems[6:12], cover2, alone
@@ -594,6 +618,29 @@
     for j in range(4):
         here = slice(j * 256, j * 256 + 256)
         e[:, here] = (dot_parts([c[:, here]], parts(diagonal2[j], 2)) * (1.0 / span)).astype(BF16)
+    if alone:
+        one = two = three = None
+    else:
+        one, two, three = (OwnerSum(place, *group) for group in groups)
+    back = dot(e[...], ct[...]).astype(BF16)
+    const = dot_parts(parts(jnp.broadcast_to(row[0:1, :], (8, 1024)), 2), [ct[...]])
+    acc[...] += dot(h2[...], back)
+
+    def dmid2(t, carry):
+        v = (acc[tile_rows(t), :] - const[0:1, :]) * s2[tile_rows(t), :]
+        store_padded(padded, t, v.astype(BF16).astype(F32))
+        return carry
+
+    lax.fori_loop(0, rows // TILE, dmid2, 0)
+    shifted_tiles(padded, columns, -1)
+    for tap in range(9):
+        here = slice(tap * 256, tap * 256 + 256)
+        value = dot(h1t[...], columns[:, here])
+        for half in range(2):
+            mid[half, here, :] = value[:, half * 128 : half * 128 + 128]
+    store_slots(groups[1][0], mid, 9, 9, 0)
+    if not alone:
+        two.swap()
     grams = parts(gram[...], 2)
     for j in range(4):
         value = dot_parts(grams, [e[:, j * 256 : j * 256 + 256]])
@@ -602,67 +649,29 @@
             here = slice(n * 128, n * 128 + 128)
             last[n] = last[n] + value[:, half * 128 : half * 128 + 128] - hsum[...] * row[0:1, here]
     store_slots(groups[0][0], last, 1, 1, 0)
-    if alone:
-        one = two = three = None
-    else:
-        one, two, three = (OwnerSum(place, *group) for group in groups)
+    if not alone:
         one.swap()
-    back = dot(e[...], c[...], ((1,), (1,))).astype(BF16)
-    const = dot_parts(parts(jnp.broadcast_to(row[0:1, :], (8, 1024)), 2), [c[...]], ((1,), (1,)))
-    acc[...] += dot(h2[...], back)
-
-    def dmid2(t, carry):
-        v = (acc[tile_rows(t), :] - const[0:1, :]) * s2[tile_rows(t), :]
-        padded[pl.ds(t * TILE + PAD, TILE), :] = v.astype(BF16).astype(F32)
-        return carry
-
-    lax.fori_loop(0, rows // TILE, dmid2, 0)
-    if not alone:
-        one.join()
-    shifted_tiles(padded, columns, -1)
-    if not alone:
-        one.combine_wide()
-    for tap in range(9):
-        here = slice(tap * 256, tap * 256 + 256)
-        value = dot(h1[...], columns[:, here], ((0,), (0,)))
-        for half in range(2):
-            mid[half, here, :] = value[:, half * 128 : half * 128 + 128]
-    target = groups[1][0]
-    store_slots(target, mid, 9, 9, 0)
-    value = pack_gains(gains)
-    for core in range(2):
-        target[slot_rows(core, 18, SLOTS[1]), :] = value[core * 128 : core * 128 + 128]
-    if not alone:
-        two.swap()
-        one.turn()
-    for tap in range(9):
-        here = slice(tap * 256, tap * 256 + 256)
-        term = dot(columns[:, here], b[here, :], ((1,), (1,)))
-        if tap == 0:
-            acc[...] = term
-        else:
-            acc[...] += term
-        if tap == 4 and not alone:
-            one.combine_thin()
+    acc[...] = dot(columns[...], bt[...])
     if not alone:
         two.join()
+        one.join()
 
     def dmid1(t, carry):
         dwhite[tile_rows(t), :256] = (acc[tile_rows(t), :] * s1[tile_rows(t), :]).astype(BF16)
         return carry
 
     lax.fori_loop(0, rows // TILE, dmid1, 0)
-    value = dot(x[...], dwhite[:, :256], ((0,), (0,)))
+    value = dot(xt[...], dwhite[:, :256])
     for half in range(2):
         top[half] = value[:, half * 128 : half * 128 + 128]
     store_slots(groups[2][0], top, 4, 4, 0)
     if not alone:
         three.swap()
         two.combine_wide()
-        one.deepen()
+        one.combine_wide()
     for j in range(4):
         here = slice(j * 256, j * 256 + 256)
-        grad_out[:, here] = (dot(dwhite[:, :256], a[here, :], ((1,), (1,))) + dpre[:, here]).astype(BF16)
+        grad_out[:, here] = (dot(dwhite[:, :256], at[:, here]) + dpre[:, here]).astype(BF16)
         if j == 1 and not alone:
             three.join()
     store = pltpu.make_async_copy(grad_out, input_grad, load_sems.at[5])
@@ -673,10 +682,13 @@
         sums[:, 32:, :] = groups[2][0][...].reshape(256, 8, 128)
     else:
         two.turn()
+        one.turn()
         three.combine_wide()
         two.combine_thin()
+        one.combine_thin()
         three.turn()
         two.deepen()
+        one.deepen()
         three.combine_thin()
         sums[0:8, :] = one.result() * scale
         three.deepen()
@@ -709,7 +721,7 @@
     scratch = [
         vmem(rows, 1024, kind=BF16), vmem(rows, 1024, kind=BF16), vmem(1024, 256, kind=BF16),
         vmem(2304, 256, kind=BF16), vmem(256, 1024, kind=BF16),
-        vmem(rows, 256), vmem(rows + 2 * PAD, 256), vmem(rows, 2304, kind=BF16),
+        vmem(rows, 256), vmem(2, rows + 2 * PAD, 128), vmem(rows, 2304, kind=BF16),
         vmem(rows, 256, kind=BF16), vmem(rows, 256), vmem(rows, 256, kind=BF16), vmem(rows, 256),
         vmem(256, 256), vmem(256, 128), vmem(256, 1024),
         vmem(16, 17, 128), vmem(16, 17, 128), vmem(16 if alone else 1, 136, 64),
@@ -719,6 +731,8 @@
         vmem(rows, 1024), vmem(rows, 1024), vmem(rows, 1024, kind=BF16), vmem(256, 1024, kind=BF16),
         vmem(256, 1024), vmem(8, 1024), vmem(8, 1024), vmem(256, 1024, kind=BF16),
         vmem(8, 256, 128), vmem(2, 2304, 128), vmem(2, 1024, 128),
+        vmem(256, rows, kind=BF16), vmem(256, rows, kind=BF16), vmem(1024, rows, kind=BF16),
+        vmem(256, 1024, kind=BF16), vmem(2304, 256, kind=BF16), vmem(1024, 256, kind=BF16),
         vmem(rows, 1024, kind=BF16), dma((6,)), *([dma((16,))] * 4 + [dma((1,))] * 2) * 2,
         *(vmem(256 * size, 128) for size in SLOTS),
         *(vmem(8, 4, 4, size, 128) for size in USED), *(vmem(8, 4, 4, size, 128) for size in USED),
@@ -738,42 +752,45 @@
     )(inputs, out_grad, conv_first, conv_middle, conv_last, gain.reshape(1, -1))
 
 
-def finish_kernel(source, sums, target, first, middle, last, gain, buffer, arrive, leave):
+def finish_kernel(source, sums, target, first, middle, last, gain, buffer, small, arrive, leave):
     count = buffer.shape[0]
     size = source.shape[0] // count
-
-    def copies(n):
-        rows = pl.ds(n * size, size)
-        return (
-            pltpu.make_async_copy(source.at[rows], buffer.at[n], arrive.at[n]),
-            pltpu.make_async_copy(buffer.at[n], target.at[rows], leave.at[n]),
-        )
-
+    spans = [pl.ds(n * size, size) for n in range(count)]
+    into = [pltpu.make_async_copy(source.at[rows], buffer.at[n], arrive.at[n]) for n, rows in enumerate(spans)]
+    out = [pltpu.make_async_copy(buffer.at[n], target.at[rows], leave.at[n]) for n, rows in enumerate(spans)]
+    into.append(pltpu.make_async_copy(sums, small, arrive.at[count]))
+    pieces = ((small.at[32:40], first), (small.at[8:26], middle), (small.at[0:8], last))
+    for n, (piece, place) in enumerate(pieces):
+        out.append(pltpu.make_async_copy(piece, place, leave.at[count + n]))
+    into[count].start()
     for n in range(count):
-        copies(n)[0].start()
-    last[...] = sums[0:8, :]
-    middle[...] = sums[8:26, :]
-    gain[...] = sums[26:27, :4]
-    first[...] = sums[32:40, :]
+        into[n].start()
+    into[count].wait()
+    for n in range(3):
+        out[count + n].start()
+    gain[...] = small[26:27, :4]
     for n in range(count):
-        copies(n)[0].wait()
-        copies(n)[1].start()
-    for n in range(count):
-        copies(n)[1].wait()
+        into[n].wait()
+        out[n].start()
+    for one in out:
+        one.wait()
 
 
 def finish(input_grad, sums):
     rows, width = input_grad.shape
-    count = 7
+    count = 2
     dma = pltpu.SemaphoreType.DMA
     return pl.pallas_call(
         finish_kernel,
         out_shape=(
             shape((rows, width), BF16), shape((8, 128)), shape((18, 128)), shape((8, 128)), shape((1, 4))
         ),
-        in_specs=[ANY, VM],
-        out_specs=(ANY, VM, VM, VM, VM),
-        scratch_shapes=[pltpu.VMEM((count, rows // count, width), BF16), dma((count,)), dma((count,))],
+        in_specs=[ANY, ANY],
+        out_specs=(ANY, ANY, ANY, ANY, VM),
+        scratch_shapes=[
+            pltpu.VMEM((count, rows // count, width), BF16), pltpu.VMEM((40, 128), F32), dma((count + 1,)),
+            dma((count + 3,)),
+        ],
         name="finish",
     )(input_grad, sums)
 

time: 95.1 us -> 87.6 us (0.921)
  Pallas kernels: 94.1 us -> 86.6 us
    pallas_call x1, Pallas kernels: 90.5 us -> 83.7 us  [block_step(): pl.pallas_call(body, out_shape=(shape((rows, 1024), BF16), shape((256, 40...]
where the time goes in v2:
time: 87.6 us; the launch traced here: 87.4 us
  Pallas kernels  86.6 us (99%)
    pallas_call x1, Pallas kernels, block_step(): pl.pallas_call(body, out_shape=(shape((rows, 1024), BF16), shape((256, 40...  83.7 us
    pallas_call x1, Pallas kernels, finish(): pl.pallas_call(finish_kernel, out_shape=(shape((rows, width), BF16), shap...  2.89 us

profile of v2, /device:TPU:2, one launch (start us, length us, event | category | flops | bytes accessed | tf_op | source)
XLA Modules:
  0.0 87.4 jit_solution(1029472625050255889)
XLA Ops:
  0.6 83.7 %block_step.1 = (bf16[784,1024]{1,0:T(8,128)(2,1)}, f32[40,128]{1,0:T(8,128)}) custom-call(bf16[784,1024]{1,0:T(8,128)(2,1)} %refs_0_.1, bf16[784,1024]{1,0:T(8,128)(2,1)} %refs_1_.1, bf16[1024,256]{1,0:T(8,128)(2,1)} %refs_2_.1, bf16[2304,256]{1,0:T(8,128)(2,1)} %refs_3_.1, bf16[256,1024]{1,0:T(8,128)(2,1)} %refs_4_.1, f32[1,1024]{1,0:T(1,128)} %bitcast.5), custom_call_target="tpu_custom_call" | custom-call | tf_op jit(solution)/shard_map/block_step/pallas_call | solution.py:744
  84.4 2.9 %finish.1 = (bf16[784,1024]{1,0:T(8,128)(2,1)}, f32[8,128]{1,0:T(8,128)}, f32[18,128]{1,0:T(8,128)}, f32[8,128]{1,0:T(8,128)}, f32[1,4]{1,0:T(1,128)}) custom-call(bf16[784,1024]{1,0:T(8,128)(2,1)} %get-tuple-element.12.source, f32[40,128]{1,0:T(8,128)} %get-tuple-element.13.sums), custom_call_target="tpu_custom_call" | custom-call | tf_op jit(solution)/shard_map/finish/pallas_call | solution.py:783

commit v3 on v2

--- a/solution.py
+++ b/solution.py
@@ -65,25 +65,41 @@
         padded[half, pl.ds(t * TILE + PAD, TILE), :] = value[:, half * 128 : half * 128 + 128]
 
 
-def shifted_tiles(padded, columns, sign):
+def shifted_columns(padded, columns, sign):
     for t in range(columns.shape[0] // TILE):
-        line, column = edges(t)
-        at = slice(t * TILE, t * TILE + TILE)
-        for tap in range(9):
-            dr, dc = sign * (tap // 3 - 1), sign * (tap % 3 - 1)
-            start = t * TILE + PAD + dr * SIDE + dc
-            keep = None
-            if dr:
-                keep = line > 0.5 if dr < 0 else line < SIDE - 1.5
-            if dc:
-                side = column > 0.5 if dc < 0 else column < SIDE - 1.5
-                keep = side if keep is None else keep & side
+        column = edges(t)[1]
+        for c in range(3):
+            dc = sign * (c - 1)
+            start = t * TILE + PAD + dc
             for half in range(2):
                 value = padded[half, start : start + TILE, :]
-                if keep is not None:
-                    value = jnp.where(keep, value, 0.0)
-                lanes = tap * 256 + half * 128
-                columns[at, lanes : lanes + 128] = value.astype(BF16)
+                if dc:
+                    value = jnp.where(column > 0.5 if dc < 0 else column < SIDE - 1.5, value, 0.0)
+                lanes = c * 256 + half * 128
+                columns[t * TILE : t * TILE + TILE, lanes : lanes + 128] = value.astype(BF16)
+
+
+def from_line(padded, half, t, dr):
+    line = edges(t)[0]
+    start = t * TILE + PAD + dr * SIDE
+    value = padded[half, start : start + TILE, :]
+    return jnp.where(line > 0.5 if dr < 0 else line < SIDE - 1.5, value, 0.0)
+
+
+def three_lines(columns, weights, acc, beside):
+    rows = columns.shape[0]
+    for r in range(3):
+        value = dot(columns[...], weights[r * 768 : r * 768 + 768, :])
+        if r == 1:
+            acc[...] = value
+        else:
+            for half in range(2):
+                beside[r // 2, half, PAD : PAD + rows, :] = value[:, half * 128 : half * 128 + 128]
+
+
+def summed_lines(acc, beside, half, t, sign):
+    value = acc[t * TILE : t * TILE + TILE, half * 128 : half * 128 + 128]
+    return value + from_line(beside.at[0], half, t, -sign) + from_line(beside.at[1], half, t, sign)
 
 
 def lanes_of(rows, right):
@@ -368,6 +384,29 @@
             one.wait_send()
 
 
+class DirectSum:
+    def __init__(self, chunk, me, peer, box, sems, at):
+        self.chunk, self.me, self.box = chunk, me, box
+        self.copies = [remote(chunk((me + s) % 4), box.at[s], sems, at + s, peer(s)) for s in range(1, 4)]
+
+    def begin(self):
+        for one in self.copies:
+            one.start()
+
+    def combine(self):
+        pass
+
+    def end(self, store):
+        for one in self.copies:
+            one.wait_recv()
+        for n in range(4):
+            store(n, self.chunk(self.me)[n] + self.box[1, n] + self.box[2, n] + self.box[3, n])
+
+    def drain(self):
+        for one in self.copies:
+            one.wait_send()
+
+
 class OwnerSum:
     def __init__(self, place, grads, other, total, half, last, wide, thin, *sems):
         self.place, self.other, self.total = place, other, total
@@ -386,10 +425,16 @@
             AxisSum(lambda d, n: total.at[2 * n : 2 * n + 2, d], place.x, place.along_x, wide.at[0], sems, 2),
             AxisSum(lambda d, n: total.at[4 + 2 * n : 6 + 2 * n, :, d], place.y, place.along_y, wide.at[1], sems, 8),
         ]
-        self.thin = [
-            AxisSum(lambda d, n: half.at[0, 2 * n : 2 * n + 2, d], place.y, place.along_y, thin.at[0], sems, 14),
-            AxisSum(lambda d, n: half.at[1, 2 * n : 2 * n + 2, d], place.x, place.along_x, thin.at[1], sems, 20),
-        ]
+        if len(thin.shape) == 5:
+            self.thin = [
+                DirectSum(lambda d: half.at[0, :, d], place.y, place.along_y, thin.at[0], sems, 14),
+                DirectSum(lambda d: half.at[1, :, d], place.x, place.along_x, thin.at[1], sems, 20),
+            ]
+        else:
+            self.thin = [
+                AxisSum(lambda d, n: half.at[0, 2 * n : 2 * n + 2, d], place.y, place.along_y, thin.at[0], sems, 14),
+                AxisSum(lambda d, n: half.at[1, 2 * n : 2 * n + 2, d], place.x, place.along_x, thin.at[1], sems, 20),
+            ]
         self.final = [
             remote(last.at[0, (place.z + s) % 8], last.at[1, s], sems, 25 + s, place.along_z(s)) for s in range(1, 8)
         ]
@@ -484,9 +529,9 @@
     x_in, og_in, a_in, b_in, c_in, gain, input_grad, sums, *scratch,
 ):
     (
-        x, og, a, b, c, acc, padded, columns, h1, s1, h2, s2, gram, hsum, wide, payload, payload2, keep, whites,
+        x, og, a, b, c, acc, padded, beside, columns, s1, twice, s2, gram, hsum, wide, payload, payload2, keep, whites,
         slopes, got, got2, mine, mine2, diagonal, diagonal2, row, white, dpre, dwhite, d, across, csum, gains, e,
-        last, mid, top, h1t, h2t, xt, at, bt, ct, grad_out, load_sems, *rest,
+        last, mid, top, h1t, h2t, xt, at, bt, ct, dmid1, grad_out, load_sems, *rest,
     ) = scratch
     sems, rest = rest[:12], rest[12:]
     groups = [rest[n :: 3] for n in range(3)]
@@ -502,6 +547,8 @@
     rows = x.shape[0]
     padded[:, :PAD, :] = jnp.zeros((2, PAD, 128), F32)
     padded[:, rows + PAD :, :] = jnp.zeros((2, PAD, 128), F32)
+    beside[:, :, :PAD, :] = jnp.zeros((2, 2, PAD, 128), F32)
+    beside[:, :, rows + PAD :, :] = jnp.zeros((2, 2, PAD, 128), F32)
 
     loads[0].wait()
     loads[1].wait()
@@ -512,23 +559,23 @@
         s = sigmoid(v)
         s1[tile_rows(t), :] = s * (1.0 + v * (1.0 - s))
         h = (v * s).astype(BF16)
-        h1[tile_rows(t), :] = h
         store_padded(padded, t, h.astype(F32))
         return carry
 
     lax.fori_loop(0, rows // TILE, first, 0)
-    shifted_tiles(padded, columns, 1)
+    shifted_columns(padded, columns, 1)
     loads[2].wait()
-    acc[...] = dot(columns[...], b[...])
-
-    def second(t, carry):
-        v = acc[tile_rows(t), :]
-        s = sigmoid(v)
-        s2[tile_rows(t), :] = s * (1.0 + v * (1.0 - s))
-        h2[tile_rows(t), :] = (v * s).astype(BF16)
-        return carry
-
-    lax.fori_loop(0, rows // TILE, second, 0)
+    three_lines(columns, b, acc, beside)
+    for t in range(rows // TILE):
+        for half in range(2):
+            here = slice(t * TILE, t * TILE + TILE), slice(half * 128, half * 128 + 128)
+            v = summed_lines(acc, beside, half, t, 1)
+            s = sigmoid(v)
+            s2[here] = s * (1.0 + v * (1.0 - s))
+            value = (v * s).astype(BF16)
+            twice[here] = value
+            twice[here[0], here[1].start + 256 : here[1].stop + 256] = value
+    h2 = twice.at[:, :256]
     h2t[...] = h2[...].T
     gram[...] = dot(h2t[...], h2[...])
     loads[3].wait()
@@ -545,7 +592,16 @@
 
     def cover():
         hsum[...] = dot(h2t[...], jnp.ones((rows, 128), BF16))
-        h1t[...] = h1[...].T
+        for r in range(3):
+            for t in range(rows // TILE):
+                for half in range(2):
+                    lanes = slice(r * 256 + half * 128, r * 256 + half * 128 + 128)
+                    if r == 1:
+                        value = padded[half, t * TILE + PAD : t * TILE + TILE + PAD, :]
+                    else:
+                        value = from_line(padded, half, t, r - 1)
+                    columns[t * TILE : t * TILE + TILE, lanes] = value.astype(BF16)
+            h1t[r * 256 : r * 256 + 256, :] = columns[:, r * 256 : r * 256 + 256].T
         for n in range(4):
             here = slice(n * 256, n * 256 + 256)
             xt[here, :] = x[:, here].T
@@ -567,7 +623,7 @@
         folded = dot_parts([c[:, here]], parts(diagonal[j], 2))
         high, low = parts(folded, 2)
         d[:, here] = high
-        white[:, here] = dot(h2[...], high) + dot(h2[...], low)
+        white[:, here] = dot(twice[...], jnp.concatenate([high, low], axis=0))
     csum[...] = jnp.zeros_like(csum)
     gains[...] = jnp.zeros_like(gains)
 
@@ -632,12 +688,15 @@
         return carry
 
     lax.fori_loop(0, rows // TILE, dmid2, 0)
-    shifted_tiles(padded, columns, -1)
-    for tap in range(9):
-        here = slice(tap * 256, tap * 256 + 256)
-        value = dot(h1t[...], columns[:, here])
-        for half in range(2):
-            mid[half, here, :] = value[:, half * 128 : half * 128 + 128]
+    shifted_columns(padded, columns, -1)
+    for column in range(3):
+        value = dot(h1t[...], columns[:, column * 256 : column * 256 + 256])
+        for r in range(3):
+            tap = 3 * r + column
+            for half in range(2):
+                mid[half, tap * 256 : tap * 256 + 256, :] = value[
+                    r * 256 : r * 256 + 256, half * 128 : half * 128 + 128
+                ]
     store_slots(groups[1][0], mid, 9, 9, 0)
     if not alone:
         two.swap()
@@ -651,17 +710,16 @@
     store_slots(groups[0][0], last, 1, 1, 0)
     if not alone:
         one.swap()
-    acc[...] = dot(columns[...], bt[...])
+    three_lines(columns, bt, acc, beside)
     if not alone:
         two.join()
         one.join()
 
-    def dmid1(t, carry):
-        dwhite[tile_rows(t), :256] = (acc[tile_rows(t), :] * s1[tile_rows(t), :]).astype(BF16)
-        return carry
-
-    lax.fori_loop(0, rows // TILE, dmid1, 0)
-    value = dot(xt[...], dwhite[:, :256])
+    for t in range(rows // TILE):
+        for half in range(2):
+            here = slice(t * TILE, t * TILE + TILE), slice(half * 128, half * 128 + 128)
+            dmid1[here] = (summed_lines(acc, beside, half, t, -1) * s1[here]).astype(BF16)
+    value = dot(xt[...], dmid1[...])
     for half in range(2):
         top[half] = value[:, half * 128 : half * 128 + 128]
     store_slots(groups[2][0], top, 4, 4, 0)
@@ -671,7 +729,7 @@
         one.combine_wide()
     for j in range(4):
         here = slice(j * 256, j * 256 + 256)
-        grad_out[:, here] = (dot(dwhite[:, :256], at[:, here]) + dpre[:, here]).astype(BF16)
+        grad_out[:, here] = (dot(dmid1[...], at[:, here]) + dpre[:, here]).astype(BF16)
         if j == 1 and not alone:
             three.join()
     store = pltpu.make_async_copy(grad_out, input_grad, load_sems.at[5])
@@ -721,8 +779,8 @@
     scratch = [
         vmem(rows, 1024, kind=BF16), vmem(rows, 1024, kind=BF16), vmem(1024, 256, kind=BF16),
         vmem(2304, 256, kind=BF16), vmem(256, 1024, kind=BF16),
-        vmem(rows, 256), vmem(2, rows + 2 * PAD, 128), vmem(rows, 2304, kind=BF16),
-        vmem(rows, 256, kind=BF16), vmem(rows, 256), vmem(rows, 256, kind=BF16), vmem(rows, 256),
+        vmem(rows, 256), vmem(2, rows + 2 * PAD, 128), vmem(2, 2, rows + 2 * PAD, 128),
+        vmem(rows, 768, kind=BF16), vmem(rows, 256), vmem(rows, 512, kind=BF16), vmem(rows, 256),
         vmem(256, 256), vmem(256, 128), vmem(256, 1024),
         vmem(16, 17, 128), vmem(16, 17, 128), vmem(16 if alone else 1, 136, 64),
         vmem(16, 17, 128), vmem(16, 17, 128), vmem(16, 17, 128), vmem(16, 17, 128),
@@ -731,13 +789,13 @@
         vmem(rows, 1024), vmem(rows, 1024), vmem(rows, 1024, kind=BF16), vmem(256, 1024, kind=BF16),
         vmem(256, 1024), vmem(8, 1024), vmem(8, 1024), vmem(256, 1024, kind=BF16),
         vmem(8, 256, 128), vmem(2, 2304, 128), vmem(2, 1024, 128),
-        vmem(256, rows, kind=BF16), vmem(256, rows, kind=BF16), vmem(1024, rows, kind=BF16),
+        vmem(768, rows, kind=BF16), vmem(256, rows, kind=BF16), vmem(1024, rows, kind=BF16),
         vmem(256, 1024, kind=BF16), vmem(2304, 256, kind=BF16), vmem(1024, 256, kind=BF16),
-        vmem(rows, 1024, kind=BF16), dma((6,)), *([dma((16,))] * 4 + [dma((1,))] * 2) * 2,
+        vmem(rows, 256, kind=BF16), vmem(rows, 1024, kind=BF16), dma((6,)), *([dma((16,))] * 4 + [dma((1,))] * 2) * 2,
         *(vmem(256 * size, 128) for size in SLOTS),
         *(vmem(8, 4, 4, size, 128) for size in USED), *(vmem(8, 4, 4, size, 128) for size in USED),
         *(vmem(2, 4, 4, size, 128) for size in USED), *(vmem(2, 8, size, 128) for size in USED),
-        *(vmem(2, 4, 2, 2, 4, size, 128) for size in USED), *(vmem(2, 4, 2, 2, size, 128) for size in USED),
+        *(vmem(2, 4, 2, 2, 4, size, 128) for size in USED), *(vmem(2, 4, 2, 2, size, 128) for size in USED[:2]), vmem(2, 4, 4, USED[2], 128),
         *[dma((33,))] * 6,
     ]
     params = {} if alone else dict(collective_id=0, has_side_effects=True)

time: 87.6 us -> 84.8 us (0.968)
  Pallas kernels: 86.6 us -> 83.8 us
    pallas_call x1, Pallas kernels: 83.7 us -> 80.9 us  [block_step(): pl.pallas_call(body, out_shape=(shape((rows, 1024), BF16), shape((256, 40...]
where the time goes in v3:
time: 84.8 us; the launch traced here: 84.6 us
  Pallas kernels  83.8 us (99%)
    pallas_call x1, Pallas kernels, block_step(): pl.pallas_call(body, out_shape=(shape((rows, 1024), BF16), shape((256, 40...  80.9 us
    pallas_call x1, Pallas kernels, finish(): pl.pallas_call(finish_kernel, out_shape=(shape((rows, width), BF16), shap...  2.89 us

profile of v3, /device:TPU:2, one launch (start us, length us, event | category | flops | bytes accessed | tf_op | source)
XLA Modules:
  0.0 84.6 jit_solution(5700787443914525888)
XLA Ops:
  0.6 80.9 %block_step.1 = (bf16[784,1024]{1,0:T(8,128)(2,1)}, f32[40,128]{1,0:T(8,128)}) custom-call(bf16[784,1024]{1,0:T(8,128)(2,1)} %refs_0_.1, bf16[784,1024]{1,0:T(8,128)(2,1)} %refs_1_.1, bf16[1024,256]{1,0:T(8,128)(2,1)} %refs_2_.1, bf16[2304,256]{1,0:T(8,128)(2,1)} %refs_3_.1, bf16[256,1024]{1,0:T(8,128)(2,1)} %refs_4_.1, f32[1,1024]{1,0:T(1,128)} %bitcast.5), custom_call_target="tpu_custom_call" | custom-call | tf_op jit(solution)/shard_map/block_step/pallas_call | solution.py:802
  81.6 2.9 %finish.1 = (bf16[784,1024]{1,0:T(8,128)(2,1)}, f32[8,128]{1,0:T(8,128)}, f32[18,128]{1,0:T(8,128)}, f32[8,128]{1,0:T(8,128)}, f32[1,4]{1,0:T(1,128)}) custom-call(bf16[784,1024]{1,0:T(8,128)(2,1)} %get-tuple-element.12.source, f32[40,128]{1,0:T(8,128)} %get-tuple-element.13.sums), custom_call_target="tpu_custom_call" | custom-call | tf_op jit(solution)/shard_map/finish/pallas_call | solution.py:841
